TPU v7x, 32 devices: a whole 2x2x4 slice. The times are simulated.
32 devices in a mesh: groups: 2 (over x), ctx: 8 (over z, y), tp: 2 (over core).
Axes of the slice: x: 2, y: 2, z: 4, core: 2. Of those that a mesh axis runs over, the one named last changes fastest.
Arguments:
- tokens: bfloat16 [8192, 2048], P(('groups', 'ctx')), parts along dimension 0, may hold values from -6 to 6
- weight: bfloat16 [2048, 3, 2048], P('ctx', None, 'tp'), may hold values from -0.125 to 0.125
- adapter_a: bfloat16 [2048, 16], replicated, may hold values from -2.390625 to 2.390625
- adapter_b: bfloat16 [16, 3, 2048], P(None, None, 'tp'), may hold values from -2.390625 to 2.390625
- short_filter: float32 [7, 3, 2048], P(None, None, 'tp'), may hold values from -1.8 to 1.8
- long_filter: float32 [128, 2048], P(None, 'tp'), may hold values from -0.54 to 0.54
- skip_gain: float32 [2048], P('tp'), may hold values from -4.2 to 4.2
- cotangent: bfloat16 [8192, 2048], P(('groups', 'ctx'), 'tp'), parts along dimension 0, may hold values from -6 to 6
Outputs:
- mixed: bfloat16 [8192, 2048], P(('groups', 'ctx'), 'tp'), parts along dimension 0
- grad_tokens: bfloat16 [8192, 2048], P(('groups', 'ctx'), 'tp'), parts along dimension 0
- grad_a: float32 [4096, 16], P('groups'), parts along dimension 0
- grad_b: float32 [32, 3, 2048], P('groups', None, 'tp'), parts along dimension 0
There are 2 independent parts, one for each index of `groups`. A program takes and returns all parts, laid end to end along the dimension named above; an argument that names none is the same for every part. Nothing has to cross between parts.
All inputs are finite; a program needn't handle non-finite values.
Results may differ from a plain program's by a relative error of at most 0.0093.
Values may be sent and summed in bfloat16 or wider, within the bound.
A program may use at most 128 MiB of HBM per device.

v0:
```python
import math
import jax
import jax.numpy as jnp
from jax import lax
from jax.sharding import PartitionSpec as P

adapter_scale = 0.03125


def shifted(value, axis, steps):
    count = lax.axis_size(axis)
    initial, last = (max(0, -steps), min(count, count - steps))
    return lax.ppermute(value, axis, [(source, source + steps) for source in range(initial, last)])


def causal(signal, filter_taps):
    return lax.conv_general_dilated(
        signal[None],
        filter_taps[::-1][:, None, :],
        (1,),
        "VALID",
        dimension_numbers=("NWC", "WIO", "NWC"),
        feature_group_count=signal.shape[1],
        precision=lax.Precision.HIGHEST,
    )[0]


def anticausal(signal, filter_taps):
    return lax.conv_general_dilated(
        signal[None],
        filter_taps[:, None, :],
        (1,),
        "VALID",
        dimension_numbers=("NWC", "WIO", "NWC"),
        feature_group_count=signal.shape[1],
        precision=lax.Precision.HIGHEST,
    )[0]


def body(tokens, weight, adapter_a, adapter_b, short_filter, long_filter, skip_gain, cotangent):
    row_count = tokens.shape[0]
    share_rows = weight.shape[0]
    channels = weight.shape[2]
    adapter_rank = adapter_a.shape[1]
    short_taps = short_filter.shape[0]
    long_taps = long_filter.shape[0]
    seq_total = row_count * lax.axis_size("ctx")
    first_row = lax.axis_index("ctx") * share_rows
    own_rows = lax.dynamic_slice_in_dim(adapter_a, first_row, share_rows, 0)
    flat_b = adapter_b.reshape(adapter_rank, 3 * channels)
    delta_w = jnp.dot(own_rows, flat_b, preferred_element_type=jnp.float32)
    merged = (
        weight.reshape(share_rows, 3 * channels).astype(jnp.float32) + adapter_scale * delta_w
    ).astype(jnp.bfloat16)
    packed = jnp.dot(
        tokens,
        lax.all_gather(merged, "ctx", axis=0, tiled=True),
        preferred_element_type=jnp.float32,
    ).astype(jnp.bfloat16)
    short_flat = short_filter.reshape(short_taps, 3 * channels)
    earlier = shifted(packed[row_count - (short_taps - 1) :], "ctx", 1)
    short_out = causal(jnp.concatenate([earlier, packed], axis=0).astype(jnp.float32), short_flat)
    query = short_out[:, :channels]
    keyed = short_out[:, channels : 2 * channels]
    valued = short_out[:, 2 * channels :]
    gated = (keyed * valued).astype(jnp.bfloat16)
    earlier_gated = shifted(gated[row_count - (long_taps - 1) :], "ctx", 1)
    gated_pad = jnp.concatenate([earlier_gated, gated], axis=0)
    filtered = causal(gated_pad.astype(jnp.float32), long_filter) + skip_gain * gated.astype(
        jnp.float32
    )
    mixed = (query * filtered).astype(jnp.bfloat16)
    cot_f = cotangent.astype(jnp.float32)
    grad_filtered = (cot_f * query).astype(jnp.bfloat16)
    later = shifted(grad_filtered[: long_taps - 1], "ctx", -1)
    grad_gated = anticausal(
        jnp.concatenate([grad_filtered, later], axis=0).astype(jnp.float32), long_filter
    ) + skip_gain * grad_filtered.astype(jnp.float32)
    grad_short = jnp.concatenate(
        [cot_f * filtered, grad_gated * valued, grad_gated * keyed], axis=1
    ).astype(jnp.bfloat16)
    later_short = shifted(grad_short[: short_taps - 1], "ctx", -1)
    grad_packed = anticausal(
        jnp.concatenate([grad_short, later_short], axis=0).astype(jnp.float32), short_flat
    ).astype(jnp.bfloat16)
    partial_grad = lax.dot_general(
        grad_packed,
        lax.all_gather(merged, "ctx", axis=0, tiled=True),
        (((1,), (1,)), ((), ())),
        preferred_element_type=jnp.float32,
    )
    grad_tokens = lax.psum_scatter(
        partial_grad.astype(jnp.bfloat16), "tp", scatter_dimension=1, tiled=True
    )
    projected = jnp.dot(tokens, adapter_a, preferred_element_type=jnp.float32).astype(jnp.bfloat16)
    part_b = lax.dot_general(
        projected, grad_packed, (((0,), (0,)), ((), ())), preferred_element_type=jnp.float32
    )
    local_through = lax.dot_general(
        grad_packed, flat_b, (((1,), (1,)), ((), ())), preferred_element_type=jnp.float32
    )
    through_b = lax.psum(local_through, "tp").astype(jnp.bfloat16)
    part_a = lax.dot_general(
        tokens, through_b, (((0,), (0,)), ((), ())), preferred_element_type=jnp.float32
    )
    sum_a, sum_b = lax.psum((part_a, part_b), "ctx")
    factor = adapter_scale / math.sqrt(seq_total)
    return (mixed, grad_tokens, sum_a * factor, (sum_b * factor).reshape(adapter_rank, 3, channels))


def solution(mesh):
    return jax.shard_map(
        body,
        mesh=mesh,
        in_specs=(
            P(("groups", "ctx"), None),
            P("ctx", None, "tp"),
            P(),
            P(None, None, "tp"),
            P(None, None, "tp"),
            P(None, "tp"),
            P("tp"),
            P(("groups", "ctx"), "tp"),
        ),
        out_specs=(
            P(("groups", "ctx"), "tp"),
            P(("groups", "ctx"), "tp"),
            P("groups", None),
            P("groups", None, "tp"),
        ),
        check_vma=False,
    )
```

profile of v0, /device:TPU:0, one launch (start us, length us, event | category | flops | bytes accessed | tf_op | source)
XLA Modules:
  0.0 450.4 jit_solution(4179814984877696524)
XLA Ops:
  8.3 2.6 copy.21
  10.9 3.3 bitcast_convert_fusion
  14.2 3.6 copy.23
  17.8 3.7 fusion.4
  21.5 179.2 %all-gather.2.cloned.1.call-done = bf16[2048,3072]{1,0:T(8,128)(2,1)} async-done(((bf16[256,3072]{1,0:T(8,128)(2,1)}), bf16[2048,3072]{1,0:T(8,128)(2,1)}) %all-gather.2.cloned.1.call-update) | async-done | bytes 12582928 | tf_op jit(solution)/shard_map/all_gather | solution.py:57
  200.7 9.6 %fusion.2 = bf16[512,3072]{1,0:T(8,128)(2,1)S(1)} fusion(bf16[512,2048]{1,0:T(8,128)(2,1)S(1)} %copy-done, bf16[2048,3072]{1,0:T(8,128)(2,1)} %all-gather.2.cloned.1.call-done), kind=kOutput, calls=%fused_computation.7 | convolution fusion | flops 6444023808 | bytes 17825792 | tf_op jit(solution)/shard_map/dot_general | solution.py:55
  212.1 2.5 collective-permute-start
  216.2 2.7 maximum_bitcast_fusion
  220.9 4.6 %reshape.28 = bf16[1,8,65,3072]{3,2,1,0:T(8,128)(2,1)} reshape(bf16[1,520,3072]{2,1,0:T(8,128)(2,1)} %pad) | data formatting | bytes 6389760 | tf_op jit(solution)/shard_map/conv_general_dilated | solution.py:17
  225.5 3.8 copy.25
  229.4 3.3 convolution_select_fusion
  232.7 6.5 %copy.26 = f32[8,65,3072]{2,1,0:T(8,128)} copy(f32[8,65,3072]{2,0,1:T(8,128)S(1)} %convolution_select_fusion) | data formatting | bytes 12779520 | tf_op jit(solution)/shard_map/conv_general_dilated | solution.py:17
  239.3 6.7 %reshape.32 = f32[1,520,3072]{2,1,0:T(8,128)} reshape(f32[8,65,3072]{2,1,0:T(8,128)} %copy.26) | data formatting | bytes 12779520 | tf_op jit(solution)/shard_map/conv_general_dilated | solution.py:17
  245.9 3.3 slice_bitcast_fusion
  249.2 2.4 fusion.24
  254.3 4.7 %rev.7 = f32[128,1024]{1,0:T(8,128)} reverse(f32[128,1024]{1,0:T(8,128)} %param.13), dimensions={0} | reverse | bytes 1048576 | tf_op jit(solution)/shard_map/rev | solution.py:19
  260.1 4.9 %collective-permute-start.1 = (bf16[127,1024]{1,0:T(8,128)(2,1)S(1)}, bf16[127,1024]{1,0:T(8,128)(2,1)S(1)}, u32[]{:S(2)}, u32[]{:S(2)}) collective-permute-start(bf16[127,1024]{1,0:T(8,128)(2,1)S(1)} %slice.38), channel_id=1, source_target_pairs={{0,2},{2,4},{4,6},{6,8},{8,10},{10,12},{12,14},{1,3},{3,5},{5,7},{... | collective-permute-start | bytes 780296 | tf_op jit(solution)/shard_map/ppermute | solution.py:13
  265.1 22.5 %fusion.17 = f32[1,512,1024]{2,0,1:T(1,128)S(1)} fusion(bf16[1,639,1024]{2,1,0:T(8,128)(2,1)S(1)} %maximum_bitcast_fusion.3, f32[128,1,1024]{2,0,1:T(8,128)S(1)} %bitcast.63), kind=kOutput, calls=%fused_computation.27 | convolution fusion | flops 805306368 | bytes 3930112 | tf_op jit(solution)/shard_map/conv_general_dilated | solution.py:29
  288.0 22.5 %fusion.19 = f32[1,512,1024]{2,0,1:T(1,128)S(1)} fusion(bf16[1,639,1024]{2,1,0:T(8,128)(2,1)S(1)} %maximum_bitcast_fusion.2, f32[128,1,1024]{2,0,1:T(8,128)S(1)} %bitcast.64), kind=kOutput, calls=%fused_computation.29 | convolution fusion | flops 805306368 | bytes 3930112 | tf_op jit(solution)/shard_map/conv_general_dilated | solution.py:17
  310.6 3.3 multiply_convert_fusion.1
  315.2 5.6 %collective-permute-done.3 = bf16[6,3072]{1,0:T(8,128)(2,1)S(1)} collective-permute-done((bf16[6,3072]{1,0:T(8,128)(2,1)S(1)}, bf16[6,3072]{1,0:T(8,128)(2,1)S(1)}, u32[]{:S(2)}, u32[]{:S(2)}) %collective-permute-start.3) | collective-permute-done | bytes 36896 | tf_op jit(solution)/shard_map/ppermute | solution.py:13
  324.6 4.6 %reshape.35 = bf16[1,8,65,3072]{3,2,1,0:T(8,128)(2,1)} reshape(bf16[1,520,3072]{2,1,0:T(8,128)(2,1)} %pad.2) | data formatting | bytes 6389760 | tf_op jit(solution)/shard_map/conv_general_dilated | solution.py:29
  329.3 3.8 copy.32
  333.1 6.1 %select_convert_fusion = bf16[8,65,3072]{2,0,1:T(8,128)(2,1)S(1)} fusion(bf16[1,7,6,3072]{3,1,2,0:T(8,128)(2,1)S(1)} %slice.40, bf16[1,8,65,3072]{3,1,2,0:T(8,128)(2,1)S(1)} %copy.32, pred[8,65]{0,1:T(8,128)(4,1)S(1)} %copy-done.13, f32[7,1,3072]{2,0,1:T(8,128)S(1)} %bitcast.70), kind=kOutput, calls=%fused_computation.3 | convolution fusion | flops 147849216 | bytes 6734344 | tf_op jit(solution)/shard_map/conv_general_dilated | solution.py:29
  339.2 3.5 copy.34
  342.7 4.7 %reshape.39 = bf16[1,520,3072]{2,1,0:T(8,128)(2,1)} reshape(bf16[8,65,3072]{2,1,0:T(8,128)(2,1)} %copy.34) | data formatting | bytes 6389760 | tf_op jit(solution)/shard_map/convert_element_type | solution.py:85
  347.5 2.9 fusion.22
  350.3 4.5 fusion.21
  354.8 4.2 psum.21
  360.1 11.9 %convolution_convert_fusion.1 = bf16[512,2048]{1,0:T(8,128)(2,1)} fusion(bf16[2048,3072]{1,0:T(8,128)(2,1)} %all-gather.2.cloned.1.call-done, bf16[1,520,3072]{2,1,0:T(8,128)(2,1)} %reshape.39), kind=kOutput, calls=%fused_computation.24 | convolution fusion | flops 6443499520 | bytes 17825792 | tf_op jit(solution)/shard_map/dot_general | solution.py:86
  372.1 59.8 %all-reduce.3.cloned.1.call-done = (f32[2048,16]{0,1:T(8,128)}, f32[16,3072]{1,0:T(8,128)}) async-done(((f32[2048,16]{0,1:T(8,128)}, f32[16,3072]{1,0:T(8,128)}), (f32[2048,16]{0,1:T(8,128)}, f32[16,3072]{1,0:T(8,128)})) %all-reduce.3.cloned.1.call-update) | async-done | bytes 327696 | tf_op jit(solution)/shard_map/psum | solution.py:106
  435.1 8.5 %reduce-scatter.2.cloned.1.call-done = bf16[512,1024]{1,0:T(8,128)(2,1)} async-done(((bf16[512,2048]{1,0:T(8,128)(2,1)}), bf16[512,1024]{1,0:T(8,128)(2,1)}) %reduce-scatter.2.cloned.1.call-update) | async-done | bytes 1048592 | tf_op jit(solution)/shard_map/reduce_scatter | solution.py:92
  (62 shorter events, 20.2 us)
Async XLA Ops:
  7.2 193.6 %copy-start = (bf16[512,2048]{1,0:T(8,128)(2,1)S(1)}, bf16[512,2048]{1,0:T(8,128)(2,1)}, u32[]{:S(2)}) copy-start(bf16[512,2048]{1,0:T(8,128)(2,1)} %param.8) | copy-start | bytes 6291460
  7.2 193.6 %all-gather.2.cloned.1.call-start = ((), (), s32[]{:S(2)}) async-start(), calls=%async_computation.1 | async-start | bytes 14155776 | tf_op jit(solution)/shard_map/all_gather | solution.py:57
  8.3 9.5 %copy-start.8 = (bf16[3,2,8,1024]{3,2,0,1:T(8,128)(2,1)}, bf16[3,2,8,1024]{3,2,0,1:T(8,128)(2,1)S(1)}, u32[]{:S(2)}) copy-start(bf16[3,2,8,1024]{3,2,0,1:T(8,128)(2,1)S(1)} %copy.39) | copy-start | bytes 294916
  21.4 193.1 %copy-start.10 = (f32[7,3,1024]{2,0,1:T(8,128)S(1)}, f32[7,3,1024]{2,0,1:T(8,128)}, u32[]{:S(2)}) copy-start(f32[7,3,1024]{2,0,1:T(8,128)} %param.12) | copy-start | bytes 258052
  21.5 410.4 %all-reduce.3.cloned.1.call-start = ((), (), s32[]{:S(2)}) async-start(), calls=%async_computation.3 | async-start | bytes 655360 | tf_op jit(solution)/shard_map/psum | solution.py:106
  210.4 1.7 copy-start.5
  212.1 4.2 collective-permute-start
  225.5 3.9 copy-start.13
  245.9 3.3 copy-start.3
  249.2 3.0 copy-start.1
  253.0 12.0 %collective-permute-start.2 = (bf16[127,1024]{1,0:T(8,128)(2,1)}, bf16[127,1024]{1,0:T(8,128)(2,1)S(1)}, u32[]{:S(2)}, u32[]{:S(2)}) collective-permute-start(bf16[127,1024]{1,0:T(8,128)(2,1)} %slice.39), channel_id=1, source_target_pairs={{2,0},{4,2},{6,4},{8,6},{10,8},{12,10},{14,12},{3,1},{5,3},{7,5},{... | collective-permute-start | bytes 780296 | tf_op jit(solution)/shard_map/ppermute | solution.py:13
  259.0 6.1 %copy-start.6 = (f32[128,1024]{1,0:T(8,128)S(1)}, f32[128,1024]{1,0:T(8,128)}, u32[]{:S(2)}) copy-start(f32[128,1024]{1,0:T(8,128)} %param.13) | copy-start | bytes 1572868
  260.1 27.6 %collective-permute-start.1 = (bf16[127,1024]{1,0:T(8,128)(2,1)S(1)}, bf16[127,1024]{1,0:T(8,128)(2,1)S(1)}, u32[]{:S(2)}, u32[]{:S(2)}) collective-permute-start(bf16[127,1024]{1,0:T(8,128)(2,1)S(1)} %slice.38), channel_id=1, source_target_pairs={{0,2},{2,4},{4,6},{6,8},{8,10},{10,12},{12,14},{1,3},{3,5},{5,7},{... | collective-permute-start | bytes 780296 | tf_op jit(solution)/shard_map/ppermute | solution.py:13
  265.1 22.6 %copy-start.2 = (bf16[512,1024]{1,0:T(8,128)(2,1)S(1)}, bf16[512,1024]{1,0:T(8,128)(2,1)}, u32[]{:S(2)}) copy-start(bf16[512,1024]{1,0:T(8,128)(2,1)} %get-tuple-element.18) | copy-start | bytes 3145732
  265.1 22.9 %copy-start.7 = (f32[128,1024]{1,0:T(8,128)S(1)}, f32[128,1024]{1,0:T(8,128)}, u32[]{:S(2)}) copy-start(f32[128,1024]{1,0:T(8,128)} %rev.7) | copy-start | bytes 1572868
  265.1 45.4 %slice-start = ((s8[6291456]{0:T(1024)(128)(4,1)}), s8[4194304]{0:T(1024)(128)(4,1)S(1)}, s32[]{:S(2)}) async-start(s8[6291456]{0:T(1024)(128)(4,1)} %bitcast.60), calls=%async_computation.4 | async-start | bytes 8388608
  287.6 22.9 %slice-start.1 = ((s8[6291456]{0:T(1024)(128)(4,1)}), s8[2097152]{0:T(1024)(128)(4,1)S(1)}, s32[]{:S(2)}) async-start(s8[6291456]{0:T(1024)(128)(4,1)} %bitcast.60), calls=%async_computation.5 | async-start | bytes 4194304
  288.0 22.6 %copy-start.4 = (bf16[512,1024]{1,0:T(8,128)(2,1)S(1)}, bf16[512,1024]{1,0:T(8,128)(2,1)}, u32[]{:S(2)}) copy-start(bf16[512,1024]{1,0:T(8,128)(2,1)} %param.15) | copy-start | bytes 3145732
  288.0 22.6 %copy-start.12 = (f32[1024]{0:T(1024)S(1)}, f32[1024]{0:T(1024)}, u32[]{:S(2)}) copy-start(f32[1024]{0:T(1024)} %param.14) | copy-start | bytes 12292
  313.9 6.9 %collective-permute-start.3 = (bf16[6,3072]{1,0:T(8,128)(2,1)S(1)}, bf16[6,3072]{1,0:T(8,128)(2,1)S(1)}, u32[]{:S(2)}, u32[]{:S(2)}) collective-permute-start(bf16[6,3072]{1,0:T(8,128)(2,1)S(1)} %pad_maximum_fusion), channel_id=1, source_target_pairs={{2,0},{4,2},{6,4},{8,6},{10,8},{12,10},{14,12},{3,1},{5,3},{7,5},{... | collective-permute-start | bytes 110600 | tf_op jit(solution)/shard_map/ppermute | solution.py:13
  342.7 4.7 %copy-start.9 = (bf16[3,2,8,1024]{3,2,0,1:T(8,128)(2,1)S(1)}, bf16[3,2,8,1024]{3,2,0,1:T(8,128)(2,1)}, u32[]{:S(2)}) copy-start(bf16[3,2,8,1024]{3,2,0,1:T(8,128)(2,1)} %copy-done.8) | copy-start | bytes 294916
  347.5 2.9 copy-start.11
  360.1 83.6 %reduce-scatter.2.cloned.1.call-start = ((), (), s32[]{:S(2)}) async-start(), calls=%async_computation.2 | async-start | bytes 3145728 | tf_op jit(solution)/shard_map/reduce_scatter | solution.py:92
Sparse Core Ops, SparseCore 0:
  21.6 179.1 all-gather.1
  360.2 71.6 all-reduce.2
  434.8 8.7 reduce-scatter.1
where the time goes:
time: 455 us; the launch traced here: 450 us
  waiting for transfers between devices  254 us (56%)
  matrix products  88.1 us (19%)
  local copies, waits for them, and re-layouts  63.5 us (14%)
  other arithmetic  16.5 us (4%)
  between operations  14.4 us (3%)
  starting transfers between devices  10 us (2%)
    all_gather x1, waiting for transfers between devices, body(): lax.all_gather(merged, 'ctx', axis=0, tiled=True)  179 us
    psum x1, waiting for transfers between devices, body(): sum_a, sum_b = lax.psum((part_a, part_b), 'ctx')  59.8 us
    conv_general_dilated x2, matrix products, anticausal(): lax.conv_general_dilated(signal[None], filter_taps[:, None, :], (1,), 'VA...  28.6 us
    conv_general_dilated x2, matrix products, causal(): lax.conv_general_dilated(signal[None], filter_taps[::-1][:, None, :], (1,...  25.8 us
    conv_general_dilated x5, local copies, waits for them, and re-layouts, causal(): lax.conv_general_dilated(signal[None], filter_taps[::-1][:, None, :], (1,...  21.7 us
    dot_general x1, matrix products, body(): lax.dot_general(grad_packed, lax.all_gather(merged, 'ctx', axis=0, tiled=...  11.9 us
    ppermute x4, starting transfers between devices, shifted(): lax.ppermute(value, axis, [(source, source + steps) for source in range(i...  9.9 us
    dot_general x1, matrix products, body(): jnp.dot(tokens, lax.all_gather(merged, 'ctx', axis=0, tiled=True), prefer...  9.63 us
  transfers between devices with their start and end apart: 7, of which 5 were waited for; matrix products, arithmetic and copies ran while one was open for 10% of the time, Pallas kernels for 0%

commit v1 on v0

--- a/solution.py
+++ b/solution.py
@@ -5,6 +5,18 @@
 from jax.sharding import PartitionSpec as P
 
 adapter_scale = 0.03125
+
+
+def doubled_up(x, axis, dim):
+    ways, here = (lax.axis_size(axis), lax.axis_index(axis))
+    grown, reach = (x, 1)
+    while reach < ways:
+        theirs = lax.ppermute(grown, axis, [(d, d ^ reach) for d in range(ways)])
+        mine_first = jnp.concatenate([grown, theirs], axis=dim)
+        theirs_first = jnp.concatenate([theirs, grown], axis=dim)
+        grown = jnp.where(here & reach == 0, mine_first, theirs_first)
+        reach = 2 * reach
+    return grown
 
 
 def shifted(value, axis, steps):
@@ -53,9 +65,7 @@
         weight.reshape(share_rows, 3 * channels).astype(jnp.float32) + adapter_scale * delta_w
     ).astype(jnp.bfloat16)
     packed = jnp.dot(
-        tokens,
-        lax.all_gather(merged, "ctx", axis=0, tiled=True),
-        preferred_element_type=jnp.float32,
+        tokens, doubled_up(merged, "ctx", 0), preferred_element_type=jnp.float32
     ).astype(jnp.bfloat16)
     short_flat = short_filter.reshape(short_taps, 3 * channels)
     earlier = shifted(packed[row_count - (short_taps - 1) :], "ctx", 1)

time: 455 us -> 831 us (1.83)
  waiting for transfers between devices: 254 us -> 602 us
  other arithmetic: 16.5 us -> 31.3 us
    ppermute x0 -> x3, waiting for transfers between devices: none -> 524 us  [doubled_up(): theirs = lax.ppermute(grown, axis, [(d, d ^ reach) for d in range(ways)])]
    all_gather x1, waiting for transfers between devices: 179 us -> 0.02 us  [body(): lax.all_gather(merged, 'ctx', axis=0, tiled=True)]
    select_n x0 -> x2, other arithmetic: none -> 14.1 us  [doubled_up(): grown = jnp.where(here & reach == 0, mine_first, theirs_first)]
  transfers between devices with their start and end apart: 7 -> 10, of which waited for: 5 -> 8; matrix products, arithmetic and copies ran while one was open for 10% -> 19% of each run, Pallas kernels for 0% -> 0%
where the time goes in v1:
time: 831 us; the launch traced here: 825 us
  waiting for transfers between devices  602 us (72%)
  matrix products  91.5 us (11%)
  local copies, waits for them, and re-layouts  64.4 us (8%)
  other arithmetic  31.3 us (4%)
  starting transfers between devices  17.2 us (2%)
  between operations  14.4 us (2%)
    ppermute x3, waiting for transfers between devices, doubled_up(): theirs = lax.ppermute(grown, axis, [(d, d ^ reach) for d in range(ways)])  524 us
    psum x1, waiting for transfers between devices, body(): sum_a, sum_b = lax.psum((part_a, part_b), 'ctx')  61 us
    conv_general_dilated x2, matrix products, anticausal(): lax.conv_general_dilated(signal[None], filter_taps[:, None, :], (1,), 'VA...  28.6 us
    conv_general_dilated x2, matrix products, causal(): lax.conv_general_dilated(signal[None], filter_taps[::-1][:, None, :], (1,...  25.8 us
    conv_general_dilated x5, local copies, waits for them, and re-layouts, causal(): lax.conv_general_dilated(signal[None], filter_taps[::-1][:, None, :], (1,...  21.7 us
  transfers between devices with their start and end apart: 10, of which 8 were waited for; matrix products, arithmetic and copies ran while one was open for 19% of the time, Pallas kernels for 0%

profile of v1, /device:TPU:0, one launch (start us, length us, event | category | flops | bytes accessed | tf_op | source)
XLA Modules:
  0.0 825.0 jit_solution(1117510094487951245)
XLA Ops:
  10.9 3.3 bitcast_convert_fusion
  14.2 3.6 copy.23
  17.8 3.7 fusion.12
  24.5 34.7 %collective-permute-done = bf16[256,3072]{1,0:T(8,128)(2,1)} collective-permute-done((bf16[256,3072]{1,0:T(8,128)(2,1)}, bf16[256,3072]{1,0:T(8,128)(2,1)}, u32[]{:S(2)}, u32[]{:S(2)}) %collective-permute-start) | collective-permute-done | bytes 1572896 | tf_op jit(solution)/shard_map/ppermute | solution.py:14
  59.2 4.5 maximum_select_fusion.7
  65.4 67.8 %collective-permute-done.1 = bf16[512,3072]{1,0:T(8,128)(2,1)} collective-permute-done((bf16[512,3072]{1,0:T(8,128)(2,1)}, bf16[512,3072]{1,0:T(8,128)(2,1)}, u32[]{:S(2)}, u32[]{:S(2)}) %collective-permute-start.1) | collective-permute-done | bytes 3145760 | tf_op jit(solution)/shard_map/ppermute | solution.py:14
  133.2 9.6 %maximum_select_fusion.2 = bf16[1024,3072]{1,0:T(8,128)(2,1)} fusion(bf16[512,3072]{1,0:T(8,128)(2,1)} %collective-permute-done.1, bf16[512,3072]{1,0:T(8,128)(2,1)} %maximum_select_fusion.7, pred[]{:T(512)S(6)} %eq.10), kind=kLoop, calls=%fused_computation.13 | loop fusion | flops 28311552 | bytes 12582913 | tf_op jit(solution)/shard_map/jit(_where)/select_n | solution.py:17
  145.4 421.4 %collective-permute-done.2 = bf16[1024,3072]{1,0:T(8,128)(2,1)} collective-permute-done((bf16[1024,3072]{1,0:T(8,128)(2,1)}, bf16[1024,3072]{1,0:T(8,128)(2,1)}, u32[]{:S(2)}, u32[]{:S(2)}) %collective-permute-start.2) | collective-permute-done | bytes 6291488 | tf_op jit(solution)/shard_map/ppermute | solution.py:14
  566.9 13.0 %fusion.10 = bf16[512,3072]{1,0:T(8,128)(2,1)} fusion(bf16[512,2048]{1,0:T(8,128)(2,1)S(1)} %copy-done, bf16[1024,3072]{1,0:T(8,128)(2,1)} %collective-permute-done.2, bf16[1024,3072]{1,0:T(8,128)(2,1)} %maximum_select_fusion.2, pred[]{:T(512)S(6)} %eq.9), kind=kOutput, calls=%fused_computation.16 | convolution fusion | flops 6500646912 | bytes 17825792 | tf_op jit(solution)/shard_map/dot_general | solution.py:67
  580.7 3.0 collective-permute-start.3
  590.0 4.6 reshape.28
  594.7 3.8 copy.25
  598.6 3.3 convolution_select_fusion
  601.9 6.5 copy.26
  608.4 6.7 reshape.32
  615.1 3.3 slice_bitcast_fusion
  622.8 4.2 collective-permute-start.4
  629.0 4.7 rev.7
  637.6 22.5 %fusion.27 = f32[1,512,1024]{2,0,1:T(1,128)S(1)} fusion(bf16[1,639,1024]{2,1,0:T(8,128)(2,1)S(1)} %maximum_bitcast_fusion.2, f32[128,1,1024]{2,0,1:T(8,128)S(1)} %bitcast.63), kind=kOutput, calls=%fused_computation.39 | convolution fusion | flops 805306368 | bytes 3930112 | tf_op jit(solution)/shard_map/conv_general_dilated | solution.py:29
  660.1 22.5 %fusion.25 = f32[1,512,1024]{2,0,1:T(1,128)S(1)} fusion(bf16[1,639,1024]{2,1,0:T(8,128)(2,1)S(1)} %maximum_bitcast_fusion.3, f32[128,1,1024]{2,0,1:T(8,128)S(1)} %bitcast.62), kind=kOutput, calls=%fused_computation.37 | convolution fusion | flops 805306368 | bytes 3930112 | tf_op jit(solution)/shard_map/conv_general_dilated | solution.py:41
  682.7 3.3 multiply_convert_fusion.1
  687.3 6.9 collective-permute-done.6
  698.1 4.6 reshape.35
  702.7 3.8 copy.32
  706.6 6.1 select_convert_fusion
  712.6 3.5 copy.34
  716.2 4.7 reshape.39
  723.8 4.2 psum.21
  729.0 4.5 fusion.29
  733.6 11.9 %convolution_convert_fusion = bf16[512,2048]{1,0:T(8,128)(2,1)} fusion(bf16[2048,3072]{1,0:T(8,128)(2,1)} %all-gather.2.cloned.1.call-done, bf16[1,520,3072]{2,1,0:T(8,128)(2,1)} %reshape.39), kind=kOutput, calls=%fused_computation.34 | convolution fusion | flops 6443499520 | bytes 17825792 | tf_op jit(solution)/shard_map/dot_general | solution.py:96
  745.5 61.0 %all-reduce.3.cloned.1.call-done = (f32[2048,16]{0,1:T(8,128)}, f32[16,3072]{1,0:T(8,128)}) async-done(((f32[2048,16]{0,1:T(8,128)}, f32[16,3072]{1,0:T(8,128)}), (f32[2048,16]{0,1:T(8,128)}, f32[16,3072]{1,0:T(8,128)})) %all-reduce.3.cloned.1.call-update) | async-done | bytes 327696 | tf_op jit(solution)/shard_map/psum | solution.py:116
  809.7 8.5 %reduce-scatter.2.cloned.1.call-done = bf16[512,1024]{1,0:T(8,128)(2,1)} async-done(((bf16[512,2048]{1,0:T(8,128)(2,1)}), bf16[512,1024]{1,0:T(8,128)(2,1)}) %reduce-scatter.2.cloned.1.call-update) | async-done | bytes 1048592 | tf_op jit(solution)/shard_map/reduce_scatter | solution.py:102
  (70 shorter events, 40.8 us)
Async XLA Ops:
  7.2 559.7 %copy-start = (bf16[512,2048]{1,0:T(8,128)(2,1)S(1)}, bf16[512,2048]{1,0:T(8,128)(2,1)}, u32[]{:S(2)}) copy-start(bf16[512,2048]{1,0:T(8,128)(2,1)} %param.8) | copy-start | bytes 6291460
  7.2 726.4 %all-gather.2.cloned.1.call-start = ((), (), s32[]{:S(2)}) async-start(), calls=%async_computation.1 | async-start | bytes 14155776 | tf_op jit(solution)/shard_map/all_gather | solution.py:98
  8.3 9.5 %copy-start.8 = (bf16[3,2,8,1024]{3,2,0,1:T(8,128)(2,1)}, bf16[3,2,8,1024]{3,2,0,1:T(8,128)(2,1)S(1)}, u32[]{:S(2)}) copy-start(bf16[3,2,8,1024]{3,2,0,1:T(8,128)(2,1)S(1)} %copy.39) | copy-start | bytes 294916
  21.5 37.7 %collective-permute-start = (bf16[256,3072]{1,0:T(8,128)(2,1)}, bf16[256,3072]{1,0:T(8,128)(2,1)}, u32[]{:S(2)}, u32[]{:S(2)}) collective-permute-start(bf16[256,3072]{1,0:T(8,128)(2,1)} %fusion.12), channel_id=1, source_target_pairs={{0,2},{2,0},{4,6},{6,4},{8,10},{10,8},{12,14},{14,12},{1,3},{3,1},... | collective-permute-start | bytes 4718600 | tf_op jit(solution)/shard_map/ppermute | solution.py:14
  63.6 69.6 %collective-permute-start.1 = (bf16[512,3072]{1,0:T(8,128)(2,1)}, bf16[512,3072]{1,0:T(8,128)(2,1)}, u32[]{:S(2)}, u32[]{:S(2)}) collective-permute-start(bf16[512,3072]{1,0:T(8,128)(2,1)} %maximum_select_fusion.7), channel_id=1, source_target_pairs={{0,4},{2,6},{4,0},{6,2},{8,12},{10,14},{12,8},{14,10},{1,5},{3,7},... | collective-permute-start | bytes 9437192 | tf_op jit(solution)/shard_map/ppermute | solution.py:14
  142.9 424.0 %collective-permute-start.2 = (bf16[1024,3072]{1,0:T(8,128)(2,1)}, bf16[1024,3072]{1,0:T(8,128)(2,1)}, u32[]{:S(2)}, u32[]{:S(2)}) collective-permute-start(bf16[1024,3072]{1,0:T(8,128)(2,1)} %maximum_select_fusion.2), channel_id=1, source_target_pairs={{0,8},{2,10},{4,12},{6,14},{8,0},{10,2},{12,4},{14,6},{1,9},{3,11}... | collective-permute-start | bytes 18874376 | tf_op jit(solution)/shard_map/ppermute | solution.py:14
  145.4 661.1 %all-reduce.3.cloned.1.call-start = ((), (), s32[]{:S(2)}) async-start(), calls=%async_computation.3 | async-start | bytes 655360 | tf_op jit(solution)/shard_map/psum | solution.py:116
  145.4 438.3 %copy-start.10 = (f32[7,3,1024]{2,0,1:T(8,128)S(1)}, f32[7,3,1024]{2,0,1:T(8,128)}, u32[]{:S(2)}) copy-start(f32[7,3,1024]{2,0,1:T(8,128)} %param.12) | copy-start | bytes 258052
  580.7 4.8 collective-permute-start.3
  594.7 3.9 copy-start.13
  615.1 3.3 copy-start.4
  618.4 2.6 copy-start.1
  621.0 1.0 copy-start.2
  622.8 11.0 %collective-permute-start.4 = (bf16[127,1024]{1,0:T(8,128)(2,1)}, bf16[127,1024]{1,0:T(8,128)(2,1)S(1)}, u32[]{:S(2)}, u32[]{:S(2)}) collective-permute-start(bf16[127,1024]{1,0:T(8,128)(2,1)} %slice.38), channel_id=1, source_target_pairs={{0,2},{2,4},{4,6},{6,8},{8,10},{10,12},{12,14},{1,3},{3,5},{5,7},{... | collective-permute-start | bytes 780296 | tf_op jit(solution)/shard_map/ppermute | solution.py:25
  627.7 8.7 %collective-permute-start.5 = (bf16[127,1024]{1,0:T(8,128)(2,1)}, bf16[127,1024]{1,0:T(8,128)(2,1)}, u32[]{:S(2)}, u32[]{:S(2)}) collective-permute-start(bf16[127,1024]{1,0:T(8,128)(2,1)} %slice.39), channel_id=1, source_target_pairs={{2,0},{4,2},{6,4},{8,6},{10,8},{12,10},{14,12},{3,1},{5,3},{7,5},{... | collective-permute-start | bytes 780296 | tf_op jit(solution)/shard_map/ppermute | solution.py:25
  633.8 3.8 copy-start.7
  637.5 22.6 %copy-start.6 = (f32[128,1024]{1,0:T(8,128)S(1)}, f32[128,1024]{1,0:T(8,128)}, u32[]{:S(2)}) copy-start(f32[128,1024]{1,0:T(8,128)} %param.13) | copy-start | bytes 1572868
  637.5 45.1 %slice-start = ((s8[6291456]{0:T(1024)(128)(4,1)}), s8[4194304]{0:T(1024)(128)(4,1)S(1)}, s32[]{:S(2)}) async-start(s8[6291456]{0:T(1024)(128)(4,1)} %bitcast.59), calls=%async_computation.4 | async-start | bytes 8388608
  660.1 22.6 %slice-start.1 = ((s8[6291456]{0:T(1024)(128)(4,1)}), s8[2097152]{0:T(1024)(128)(4,1)S(1)}, s32[]{:S(2)}) async-start(s8[6291456]{0:T(1024)(128)(4,1)} %bitcast.59), calls=%async_computation.5 | async-start | bytes 4194304
  660.1 22.6 %copy-start.3 = (bf16[512,1024]{1,0:T(8,128)(2,1)S(1)}, bf16[512,1024]{1,0:T(8,128)(2,1)}, u32[]{:S(2)}) copy-start(bf16[512,1024]{1,0:T(8,128)(2,1)} %copy-done.2) | copy-start | bytes 3145732
  660.1 22.6 %copy-start.5 = (bf16[512,1024]{1,0:T(8,128)(2,1)S(1)}, bf16[512,1024]{1,0:T(8,128)(2,1)}, u32[]{:S(2)}) copy-start(bf16[512,1024]{1,0:T(8,128)(2,1)} %param.15) | copy-start | bytes 3145732
  660.1 22.6 %copy-start.12 = (f32[1024]{0:T(1024)S(1)}, f32[1024]{0:T(1024)}, u32[]{:S(2)}) copy-start(f32[1024]{0:T(1024)} %param.14) | copy-start | bytes 12292
  686.0 8.2 collective-permute-start.6
  716.2 4.7 copy-start.9
  720.9 8.1 copy-start.11
  733.5 84.7 %reduce-scatter.2.cloned.1.call-start = ((), (), s32[]{:S(2)}) async-start(), calls=%async_computation.2 | async-start | bytes 3145728 | tf_op jit(solution)/shard_map/reduce_scatter | solution.py:102
Sparse Core Ops, SparseCore 0:
  145.5 372.3 all-gather.1
  733.7 72.7 all-reduce.2
  809.4 8.7 reduce-scatter.1
